TPU v7x, 256 devices: a whole 4x4x8 slice. The times are simulated.
256 devices in a mesh: dp: 32 (over z, y), tensor: 8 (over x, core).
Axes of the slice: x: 4, y: 4, z: 8, core: 2. Of those that a mesh axis runs over, the one named last changes fastest.
Arguments:
- hidden: bfloat16 [4096, 26624], P('dp', 'tensor'), may hold values from -6 to 6
- out_grad: bfloat16 [4096, 8192], P(('dp', 'tensor')), may hold values from -0.375 to 0.375
- master: float32 [8192, 26624], P('dp', 'tensor'), may hold values from -0.3125 to 0.3125
- first_moment: bfloat16 [8192, 26624], P('dp', 'tensor'), may hold values from -4 to 4
- second_moment: bfloat16 [8192, 26624], P('dp', 'tensor'), may hold values from 0.049804688 to 1
- row_counts: int32 [8], replicated, may hold values from 2816 to 3840, as said below
- step_count: int32 [1], replicated, may hold values from 1 to 11
Outputs:
- adam_update: float32 [8192, 26624], P('dp', 'tensor')
- weights_tp: bfloat16 [8192, 30720], P('dp', 'tensor')
Inputs may be any that keep to these rules, and one draw needn't show every extreme that they name: Tensor index j takes row_counts[j] consecutive hidden units in order; they sum to 26624; offsets[j] differs from j * 3328 by at most 256; the largest count equals 3840.
All inputs are finite; a program needn't handle non-finite values.
Results may differ from a plain program's by a relative error of at most 0.0045.
Values may be sent and summed in bfloat16 or wider, within the bound.
No kernel may reach another device: no remote copies, remote signals or barrier semaphores. Data moves between devices by JAX's collectives and lax.ppermute only.
A program may use at most 192 MiB of HBM per device.

v0:
```python
import jax
import jax.numpy as jnp
import numpy as np
from jax import lax
from jax.sharding import Mesh, PartitionSpec as P

DRIFT = 256
CAP = 3840
CHUNKS = ((0, 896), (2432, 3328), (896, 1664), (1664, 2432))
beta_first = 0.9
beta_second = 0.95
epsilon = 1e-08
decay_rate = 0.1
learn_rate = 0.001
TENSOR = ("x", "core")


def adamw(gradient, master, first_moment, second_moment, first_fix, second_fix):
    first_new = beta_first * first_moment + (1.0 - beta_first) * gradient
    second_new = beta_second * second_moment + (1.0 - beta_second) * gradient * gradient
    update = (
        first_new / first_fix / (jnp.sqrt(second_new / second_fix) + epsilon) + decay_rate * master
    )
    master_new = master - learn_rate * update
    return (master_new, update)


def per_device(hidden, out_grad, master, first_moment, second_moment, row_counts, step_count):
    width = hidden.shape[1]
    tensor_count = lax.axis_size(TENSOR)
    z_count = lax.axis_size("z")
    local_tokens = out_grad.shape[0]
    features = out_grad.shape[1] // z_count
    regrouped = lax.all_to_all(out_grad, "z", split_axis=1, concat_axis=0, tiled=True)
    spread = lax.all_gather(regrouped, TENSOR, axis=0, tiled=True)
    cotangent = spread.reshape(tensor_count, z_count, local_tokens, features)
    cotangent = cotangent.transpose(1, 0, 2, 3).reshape(-1, features)
    steps_done = step_count[0].astype(jnp.float32)
    first_fix = 1.0 - jnp.power(beta_first, steps_done)
    second_fix = 1.0 - jnp.power(beta_second, steps_done)
    gathered = [
        lax.all_gather(hidden[:, low:high], "z", axis=0, tiled=True) for low, high in CHUNKS
    ]
    updates = {}
    weights = {}
    for (low, high), acts in zip(CHUNKS, gathered):
        partial_value = lax.dot_general(
            cotangent, acts, (((0,), (0,)), ((), ())), preferred_element_type=jnp.float32
        ).astype(jnp.bfloat16)
        gradient = lax.psum_scatter(partial_value, "y", scatter_dimension=0, tiled=True)
        master_new, update = adamw(
            gradient.astype(jnp.float32),
            master[:, low:high],
            first_moment[:, low:high].astype(jnp.float32),
            second_moment[:, low:high].astype(jnp.float32),
            first_fix,
            second_fix,
        )
        updates[low] = update
        weights[low] = master_new.astype(jnp.bfloat16)
    order = sorted(updates)
    head = weights[order[0]][:, :DRIFT]
    tail = weights[order[-1]][:, -DRIFT:]
    ends = tensor_count - 1
    left = lax.ppermute(tail, TENSOR, [(i, i + 1) for i in range(ends)])
    right = lax.ppermute(head, TENSOR, [(i + 1, i) for i in range(ends)])
    position = lax.axis_index(TENSOR)
    places = jnp.arange(tensor_count, dtype=jnp.int32)
    first_slot = jnp.sum(jnp.where(places < position, row_counts, 0))
    length = jnp.sum(jnp.where(places == position, row_counts, 0))
    rows = master.shape[0]
    widened = jnp.concatenate(
        [left] + [weights[k] for k in order] + [right, jnp.zeros((rows, 2 * DRIFT), jnp.bfloat16)],
        axis=1,
    )
    start = first_slot - position * width + DRIFT
    window = lax.dynamic_slice_in_dim(widened, start, CAP, 1)
    slot_index = jnp.arange(CAP, dtype=jnp.int32)
    laid = jnp.where((slot_index < length)[None, :], window, jnp.zeros((), jnp.bfloat16))
    return (jnp.concatenate([updates[k] for k in order], axis=1), laid)


def solution(mesh):
    fine = Mesh(np.asarray(mesh.devices).reshape(8, 4, 4, 2), ("z", "y", "x", "core"))
    dp = ("z", "y")
    return jax.shard_map(
        per_device,
        mesh=fine,
        in_specs=(
            P(dp, TENSOR),
            P(dp + TENSOR, None),
            P(dp, TENSOR),
            P(dp, TENSOR),
            P(dp, TENSOR),
            P(),
            P(),
        ),
        out_specs=(P(dp, TENSOR), P(dp, TENSOR)),
        check_vma=False,
    )
```

profile of v0, /device:TPU:2, one launch (start us, length us, event | category | flops | bytes accessed | tf_op | source)
XLA Modules:
  0.0 358.5 jit_solution(4531047940108893145)
XLA Ops:
  8.2 20.2 %all_to_all.19 = bf16[16,8,1024]{2,0,1:T(8,128)(2,1)} all-to-all(bf16[16,8,1024]{2,0,1:T(8,128)(2,1)S(1)} %bitcast.27), channel_id=1, replica_groups=mesh['z'=8,'y'=4,'x'=4,'core'=2] {'z'}, dimensions={1} | all-to-all | bytes 524288 | tf_op jit(solution)/shard_map/all_to_all | solution.py:34
  28.5 1.9 fusion.41
  33.6 18.1 %all-gather.6.cloned.1.call-done = bf16[1024,1024]{1,0:T(8,128)(2,1)} async-done(((bf16[128,1024]{1,0:T(8,128)(2,1)}), bf16[1024,1024]{1,0:T(8,128)(2,1)}) %all-gather.6.cloned.1.call-update) | async-done | bytes 2097168 | tf_op jit(solution)/shard_map/all_gather | solution.py:35
  53.5 42.4 %all-gather.14.cloned.1.call-done = bf16[1024,896]{1,0:T(8,128)(2,1)} async-done(((bf16[128,896]{1,0:T(8,128)(2,1)}), bf16[1024,896]{1,0:T(8,128)(2,1)}) %all-gather.14.cloned.1.call-update) | async-done | bytes 1835024 | tf_op jit(solution)/shard_map/all_gather | solution.py:42
  95.9 5.1 %convolution_convert_fusion = bf16[1024,896]{1,0:T(8,128)(2,1)} fusion(bf16[1024,1024]{1,0:T(8,128)(2,1)S(1)} %bitcast.22, bf16[1024,896]{1,0:T(8,128)(2,1)} %all-gather.14.cloned.1.call-done), kind=kOutput, calls=%fused_computation.2 | convolution fusion | flops 1879965696 | bytes 5767168 | tf_op jit(solution)/shard_map/dot_general | solution.py:47
  101.1 36.4 %all-gather.8.cloned.1.call-done = bf16[1024,896]{1,0:T(8,128)(2,1)} async-done(((bf16[128,896]{1,0:T(8,128)(2,1)}), bf16[1024,896]{1,0:T(8,128)(2,1)}) %all-gather.8.cloned.1.call-update) | async-done | bytes 1835024 | tf_op jit(solution)/shard_map/all_gather | solution.py:42
  137.5 5.1 %convolution_convert_fusion.1 = bf16[1024,896]{1,0:T(8,128)(2,1)} fusion(bf16[1024,1024]{1,0:T(8,128)(2,1)S(1)} %bitcast.23, bf16[1024,896]{1,0:T(8,128)(2,1)} %all-gather.8.cloned.1.call-done), kind=kOutput, calls=%fused_computation.3 | convolution fusion | flops 1879965696 | bytes 5767168 | tf_op jit(solution)/shard_map/dot_general | solution.py:47
  142.7 35.1 %all-gather.10.cloned.1.call-done = bf16[1024,768]{1,0:T(8,128)(2,1)} async-done(((bf16[128,768]{1,0:T(8,128)(2,1)}), bf16[1024,768]{1,0:T(8,128)(2,1)}) %all-gather.10.cloned.1.call-update) | async-done | bytes 1572880 | tf_op jit(solution)/shard_map/all_gather | solution.py:42
  177.7 4.4 %convolution_convert_fusion.3 = bf16[1024,768]{1,0:T(8,128)(2,1)} fusion(bf16[1024,1024]{1,0:T(8,128)(2,1)S(1)} %bitcast.24, bf16[1024,768]{1,0:T(8,128)(2,1)} %all-gather.10.cloned.1.call-done), kind=kOutput, calls=%fused_computation.5 | convolution fusion | flops 1611399168 | bytes 5242880 | tf_op jit(solution)/shard_map/dot_general | solution.py:47
  182.2 35.8 %all-gather.12.cloned.1.call-done = bf16[1024,768]{1,0:T(8,128)(2,1)} async-done(((bf16[128,768]{1,0:T(8,128)(2,1)}), bf16[1024,768]{1,0:T(8,128)(2,1)}) %all-gather.12.cloned.1.call-update) | async-done | bytes 1572880 | tf_op jit(solution)/shard_map/all_gather | solution.py:42
  218.0 4.4 %convolution_convert_fusion.2 = bf16[1024,768]{1,0:T(8,128)(2,1)} fusion(bf16[1024,1024]{1,0:T(8,128)(2,1)S(1)} %bitcast.25, bf16[1024,768]{1,0:T(8,128)(2,1)} %all-gather.12.cloned.1.call-done), kind=kOutput, calls=%fused_computation.4 | convolution fusion | flops 1611399168 | bytes 5242880 | tf_op jit(solution)/shard_map/dot_general | solution.py:47
  223.2 26.5 %reduce-scatter.11.cloned.1.call-done = bf16[256,896]{1,0:T(8,128)(2,1)} async-done(((bf16[1024,896]{1,0:T(8,128)(2,1)}), bf16[256,896]{1,0:T(8,128)(2,1)}) %reduce-scatter.11.cloned.1.call-update) | async-done | bytes 458768 | tf_op jit(solution)/shard_map/reduce_scatter | solution.py:50
  249.8 2.4 subtract_convert_fusion.1
  252.1 1.9 collective-permute-start
  256.0 2.5 collective-permute-done
  259.1 23.7 %reduce-scatter.5.cloned.1.call-done = bf16[256,896]{1,0:T(8,128)(2,1)} async-done(((bf16[1024,896]{1,0:T(8,128)(2,1)}), bf16[256,896]{1,0:T(8,128)(2,1)}) %reduce-scatter.5.cloned.1.call-update) | async-done | bytes 458768 | tf_op jit(solution)/shard_map/reduce_scatter | solution.py:50
  282.8 3.2 constant_dynamic-update-slice_fusion.2
  286.0 2.1 collective-permute-start.1
  288.2 25.2 %reduce-scatter.7.cloned.1.call-done = bf16[256,768]{1,0:T(8,128)(2,1)} async-done(((bf16[1024,768]{1,0:T(8,128)(2,1)}), bf16[256,768]{1,0:T(8,128)(2,1)}) %reduce-scatter.7.cloned.1.call-update) | async-done | bytes 393232 | tf_op jit(solution)/shard_map/reduce_scatter | solution.py:50
  313.3 3.0 fusion.32
  316.3 27.6 %reduce-scatter.9.cloned.1.call-done = bf16[256,768]{1,0:T(8,128)(2,1)} async-done(((bf16[1024,768]{1,0:T(8,128)(2,1)}), bf16[256,768]{1,0:T(8,128)(2,1)}) %reduce-scatter.9.cloned.1.call-update) | async-done | bytes 393232 | tf_op jit(solution)/shard_map/reduce_scatter | solution.py:50
  343.9 2.9 fusion.33
  346.9 2.0 pad_maximum_fusion
  349.7 2.4 dynamic-slice_select_fusion
  (34 shorter events, 9.0 us)
Async XLA Ops:
  7.2 44.6 %all-gather.6.cloned.1.call-start = ((), (), s32[]{:S(2)}) async-start(), calls=%async_computation.5 | async-start | bytes 2359296 | tf_op jit(solution)/shard_map/all_gather | solution.py:35
  28.5 67.5 %all-gather.14.cloned.1.call-start = ((), (), s32[]{:S(2)}) async-start(), calls=%async_computation.12 | async-start | bytes 2064384 | tf_op jit(solution)/shard_map/all_gather | solution.py:42
  30.4 107.1 %all-gather.8.cloned.1.call-start = ((), (), s32[]{:S(2)}) async-start(), calls=%async_computation.6 | async-start | bytes 2064384 | tf_op jit(solution)/shard_map/all_gather | solution.py:42
  31.1 146.6 %all-gather.10.cloned.1.call-start = ((), (), s32[]{:S(2)}) async-start(), calls=%async_computation.8 | async-start | bytes 1769472 | tf_op jit(solution)/shard_map/all_gather | solution.py:42
  33.0 185.0 %all-gather.12.cloned.1.call-start = ((), (), s32[]{:S(2)}) async-start(), calls=%async_computation.10 | async-start | bytes 1769472 | tf_op jit(solution)/shard_map/all_gather | solution.py:42
  33.6 216.2 %reduce-scatter.11.cloned.1.call-start = ((), (), s32[]{:S(2)}) async-start(), calls=%async_computation.13 | async-start | bytes 2293760 | tf_op jit(solution)/shard_map/reduce_scatter | solution.py:50
  101.1 181.7 %reduce-scatter.5.cloned.1.call-start = ((), (), s32[]{:S(2)}) async-start(), calls=%async_computation.7 | async-start | bytes 2293760 | tf_op jit(solution)/shard_map/reduce_scatter | solution.py:50
  142.6 170.7 %reduce-scatter.7.cloned.1.call-start = ((), (), s32[]{:S(2)}) async-start(), calls=%async_computation.9 | async-start | bytes 1966080 | tf_op jit(solution)/shard_map/reduce_scatter | solution.py:50
  182.2 161.8 %reduce-scatter.9.cloned.1.call-start = ((), (), s32[]{:S(2)}) async-start(), calls=%async_computation.11 | async-start | bytes 1966080 | tf_op jit(solution)/shard_map/reduce_scatter | solution.py:50
  222.5 31.6 %copy-start.1 = (s32[8]{0:T(128)S(1)}, s32[8]{0:T(128)}, u32[]{:S(2)}) copy-start(s32[8]{0:T(128)} %param.12) | copy-start | bytes 100
  252.1 6.3 %collective-permute-start = (bf16[256,256]{1,0:T(8,128)(2,1)S(1)}, bf16[256,256]{1,0:T(8,128)(2,1)S(1)}, u32[]{:S(2)}, u32[]{:S(2)}) collective-permute-start(bf16[256,256]{1,0:T(8,128)(2,1)S(1)} %slice.72), channel_id=1, source_target_pairs={{0,1},{1,2},{2,3},{3,4},{4,5},{5,6},{6,7},{8,9},{9,10},{10,11},{11... | collective-permute-start | bytes 393224 | tf_op jit(solution)/shard_map/ppermute | solution.py:65
  286.0 63.6 %collective-permute-start.1 = (bf16[256,256]{1,0:T(8,128)(2,1)S(1)}, bf16[256,256]{1,0:T(8,128)(2,1)S(1)}, u32[]{:S(2)}, u32[]{:S(2)}) collective-permute-start(bf16[256,256]{1,0:T(8,128)(2,1)S(1)} %slice.73), channel_id=1, source_target_pairs={{1,0},{2,1},{3,2},{4,3},{5,4},{6,5},{7,6},{9,8},{10,9},{11,10},{12... | collective-permute-start | bytes 393224 | tf_op jit(solution)/shard_map/ppermute | solution.py:66
  346.9 2.7 copy-start
Sparse Core Ops, SparseCore 0:
  28.6 23.1 all-gather.5
  54.1 41.7 all-gather.13
  98.3 39.1 all-gather.7
  139.1 38.5 all-gather.9
  179.4 38.5 all-gather.11
  221.0 28.7 reduce-scatter.10
  252.9 29.8 reduce-scatter.4
  285.3 27.9 reduce-scatter.6
  315.9 27.9 reduce-scatter.8
where the time goes:
time: 359 us
  waiting for transfers between devices  275 us (77%)
  blocking collectives  20.2 us (6%)
  matrix products  19.1 us (5%)
  other arithmetic  17.1 us (5%)
  between operations  15.3 us (4%)
  local copies, waits for them, and re-layouts  7.9 us (2%)
  starting transfers between devices  4.42 us (1%)
    all_gather x4, waiting for transfers between devices, per_device(): lax.all_gather(hidden[:, low:high], 'z', axis=0, tiled=True)  150 us
    reduce_scatter x4, waiting for transfers between devices, per_device(): lax.psum_scatter(partial_value, 'y', scatter_dimension=0, tiled=True)  103 us
    all_to_all x1, blocking collectives, per_device(): lax.all_to_all(out_grad, 'z', split_axis=1, concat_axis=0, tiled=True)  20.2 us
    dot_general x4, matrix products, per_device(): lax.dot_general(cotangent, acts, (((0,), (0,)), ((), ())), preferred_elem...  19.1 us
    all_gather x1, waiting for transfers between devices, per_device(): spread = lax.all_gather(regrouped, TENSOR, axis=0, tiled=True)  18.1 us
    unnamed x3, other arithmetic  9.14 us
  transfers between devices with their start and end apart: 11, of which 10 were waited for; matrix products, arithmetic and copies ran while one was open for 11% of the time, Pallas kernels for 0%

commit v1 on v0

--- a/solution.py
+++ b/solution.py
@@ -13,6 +13,13 @@
 decay_rate = 0.1
 learn_rate = 0.001
 TENSOR = ("x", "core")
+
+
+def gates_process(z_in):
+    z1 = lax.psum(1, "z")
+    val = jnp.stack([z_in] * z1, axis=0)
+    n_now = lax.all_to_all(val, "z", 0, 0)
+    return jnp.concatenate(n_now, axis=0)
 
 
 def adamw(gradient, master, first_moment, second_moment, first_fix, second_fix):
@@ -38,9 +45,7 @@
     steps_done = step_count[0].astype(jnp.float32)
     first_fix = 1.0 - jnp.power(beta_first, steps_done)
     second_fix = 1.0 - jnp.power(beta_second, steps_done)
-    gathered = [
-        lax.all_gather(hidden[:, low:high], "z", axis=0, tiled=True) for low, high in CHUNKS
-    ]
+    gathered = [gates_process(hidden[:, low:high]) for low, high in CHUNKS]
     updates = {}
     weights = {}
     for (low, high), acts in zip(CHUNKS, gathered):

time: 359 us -> 266 us (0.74)
  waiting for transfers between devices: 275 us -> 124 us
  blocking collectives: 20.2 us -> 62 us
  starting transfers between devices: 4.42 us -> 17.2 us
    all_gather x4 -> x0, waiting for transfers between devices: 150 us -> none  [per_device(): lax.all_gather(hidden[:, low:high], 'z', axis=0, tiled=True)]
    all_to_all x0 -> x3, waiting for transfers between devices: none -> 99.4 us  [gates_process(): n_now = lax.all_to_all(val, 'z', 0, 0)]
    reduce_scatter x4, waiting for transfers between devices: 103 us -> 6.52 us  [per_device(): lax.psum_scatter(partial_value, 'y', scatter_dimension=0, tiled=True)]
    all_to_all x0 -> x1, blocking collectives: none -> 41.7 us  [gates_process(): n_now = lax.all_to_all(val, 'z', 0, 0)]
    all_to_all x0 -> x3, starting transfers between devices: none -> 12.9 us  [gates_process(): n_now = lax.all_to_all(val, 'z', 0, 0)]
    another operation x0 -> x4, local copies, waits for them, and re-layouts: none -> 4.29 us  [gates_process(): val = jnp.stack([z_in] * z1, axis=0)]
  transfers between devices with their start and end apart: 11 -> 10, of which waited for: 10 -> 6; matrix products, arithmetic and copies ran while one was open for 11% -> 16% of each run, Pallas kernels for 0% -> 0%
where the time goes in v1:
time: 266 us
  waiting for transfers between devices  124 us (47%)
  blocking collectives  62 us (23%)
  matrix products  19.1 us (7%)
  starting transfers between devices  17.2 us (6%)
  other arithmetic  17.1 us (6%)
  between operations  15.3 us (6%)
  local copies, waits for them, and re-layouts  10.7 us (4%)
    all_to_all x3, waiting for transfers between devices, gates_process(): n_now = lax.all_to_all(val, 'z', 0, 0)  99.4 us
    all_to_all x1, blocking collectives, gates_process(): n_now = lax.all_to_all(val, 'z', 0, 0)  41.7 us
    all_to_all x1, blocking collectives, per_device(): lax.all_to_all(out_grad, 'z', split_axis=1, concat_axis=0, tiled=True)  20.2 us
    dot_general x4, matrix products, per_device(): lax.dot_general(cotangent, acts, (((0,), (0,)), ((), ())), preferred_elem...  19.1 us
    all_gather x1, waiting for transfers between devices, per_device(): spread = lax.all_gather(regrouped, TENSOR, axis=0, tiled=True)  16 us
    all_to_all x3, starting transfers between devices, gates_process(): n_now = lax.all_to_all(val, 'z', 0, 0)  12.9 us
    unnamed x3, other arithmetic  9.12 us
    reduce_scatter x4, waiting for transfers between devices, per_device(): lax.psum_scatter(partial_value, 'y', scatter_dimension=0, tiled=True)  6.52 us
  transfers between devices with their start and end apart: 10, of which 6 were waited for; matrix products, arithmetic and copies ran while one was open for 16% of the time, Pallas kernels for 0%

profile of v1, /device:TPU:2, one launch (start us, length us, event | category | flops | bytes accessed | tf_op | source)
XLA Modules:
  0.0 265.6 jit_solution(1569552806116474736)
XLA Ops:
  8.2 20.2 %all_to_all.39 = bf16[16,8,1024]{2,0,1:T(8,128)(2,1)} all-to-all(bf16[16,8,1024]{2,0,1:T(8,128)(2,1)S(1)} %bitcast.32), channel_id=1, replica_groups=mesh['z'=8,'y'=4,'x'=4,'core'=2] {'z'}, dimensions={1} | all-to-all | bytes 524288 | tf_op jit(solution)/shard_map/all_to_all | solution.py:41
  31.0 4.3 %all-to-all-start.4 = ((bf16[8,128,896]{2,1,0:T(8,128)(2,1)}), bf16[8,128,896]{2,1,0:T(8,128)(2,1)}, u32[]{:S(2)}, u32[]{:S(2)}) async-start(bf16[8,128,896]{2,1,0:T(8,128)(2,1)} %stack.11), calls=%async_computation.7 | async-start | bytes 3670016 | tf_op jit(solution)/shard_map/all_to_all | solution.py:21
  35.3 16.0 %all-gather.2.cloned.1.call-done = bf16[1024,1024]{1,0:T(8,128)(2,1)} async-done(((bf16[128,1024]{1,0:T(8,128)(2,1)}), bf16[1024,1024]{1,0:T(8,128)(2,1)}) %all-gather.2.cloned.1.call-update) | async-done | bytes 2097168 | tf_op jit(solution)/shard_map/all_gather | solution.py:42
  51.4 1.8 copy.13
  53.2 26.2 %all-to-all-done.4 = bf16[8,128,896]{2,1,0:T(8,128)(2,1)} async-done(((bf16[8,128,896]{2,1,0:T(8,128)(2,1)}), bf16[8,128,896]{2,1,0:T(8,128)(2,1)}, u32[]{:S(2)}, u32[]{:S(2)}) %all-to-all-start.4) | async-done | bytes 1835040 | tf_op jit(solution)/shard_map/all_to_all | solution.py:21
  80.9 4.3 %all-to-all-start.1 = ((bf16[8,128,896]{2,1,0:T(8,128)(2,1)}), bf16[8,128,896]{2,1,0:T(8,128)(2,1)}, u32[]{:S(2)}, u32[]{:S(2)}) async-start(bf16[8,128,896]{2,1,0:T(8,128)(2,1)} %stack.8), calls=%async_computation.1 | async-start | bytes 3670016 | tf_op jit(solution)/shard_map/all_to_all | solution.py:21
  85.2 5.1 %convolution_convert_fusion = bf16[1024,896]{1,0:T(8,128)(2,1)} fusion(bf16[1024,1024]{1,0:T(8,128)(2,1)S(1)} %bitcast.25, bf16[1024,896]{1,0:T(8,128)(2,1)} %bitcast.11), kind=kOutput, calls=%fused_computation.2 | convolution fusion | flops 1879965696 | bytes 5767168 | tf_op jit(solution)/shard_map/dot_general | solution.py:52
  90.4 40.8 %all-to-all-done.1 = bf16[8,128,896]{2,1,0:T(8,128)(2,1)} async-done(((bf16[8,128,896]{2,1,0:T(8,128)(2,1)}), bf16[8,128,896]{2,1,0:T(8,128)(2,1)}, u32[]{:S(2)}, u32[]{:S(2)}) %all-to-all-start.1) | async-done | bytes 1835040 | tf_op jit(solution)/shard_map/all_to_all | solution.py:21
  131.2 5.1 %convolution_convert_fusion.1 = bf16[1024,896]{1,0:T(8,128)(2,1)} fusion(bf16[1024,1024]{1,0:T(8,128)(2,1)S(1)} %bitcast.26, bf16[1024,896]{1,0:T(8,128)(2,1)} %bitcast.5), kind=kOutput, calls=%fused_computation.3 | convolution fusion | flops 1879965696 | bytes 5767168 | tf_op jit(solution)/shard_map/dot_general | solution.py:52
  137.5 41.7 %all_to_all.40 = bf16[8,128,768]{2,1,0:T(8,128)(2,1)} all-to-all(bf16[8,128,768]{2,1,0:T(8,128)(2,1)S(1)} %stack.9), channel_id=1, replica_groups=mesh['z'=8,'y'=4,'x'=4,'core'=2] {'z'}, dimensions={0} | all-to-all | bytes 3145728 | tf_op jit(solution)/shard_map/all_to_all | solution.py:21
  180.5 4.3 %all-to-all-start.3 = ((bf16[8,128,768]{2,1,0:T(8,128)(2,1)}), bf16[8,128,768]{2,1,0:T(8,128)(2,1)}, u32[]{:S(2)}, u32[]{:S(2)}) async-start(bf16[8,128,768]{2,1,0:T(8,128)(2,1)} %stack.10), calls=%async_computation.5 | async-start | bytes 3145728 | tf_op jit(solution)/shard_map/all_to_all | solution.py:21
  184.9 4.4 %convolution_convert_fusion.3 = bf16[1024,768]{1,0:T(8,128)(2,1)} fusion(bf16[1024,1024]{1,0:T(8,128)(2,1)S(1)} %bitcast.27, bf16[1024,768]{1,0:T(8,128)(2,1)} %bitcast.30), kind=kOutput, calls=%fused_computation.5 | convolution fusion | flops 1611399168 | bytes 5242880 | tf_op jit(solution)/shard_map/dot_general | solution.py:52
  189.4 32.4 %all-to-all-done.3 = bf16[8,128,768]{2,1,0:T(8,128)(2,1)} async-done(((bf16[8,128,768]{2,1,0:T(8,128)(2,1)}), bf16[8,128,768]{2,1,0:T(8,128)(2,1)}, u32[]{:S(2)}, u32[]{:S(2)}) %all-to-all-start.3) | async-done | bytes 1572896 | tf_op jit(solution)/shard_map/all_to_all | solution.py:21
  221.7 4.4 %convolution_convert_fusion.2 = bf16[1024,768]{1,0:T(8,128)(2,1)} fusion(bf16[1024,1024]{1,0:T(8,128)(2,1)S(1)} %bitcast.28, bf16[1024,768]{1,0:T(8,128)(2,1)} %bitcast.10), kind=kOutput, calls=%fused_computation.4 | convolution fusion | flops 1611399168 | bytes 5242880 | tf_op jit(solution)/shard_map/dot_general | solution.py:52
  227.0 2.4 subtract_convert_fusion.1
  229.4 2.1 collective-permute-start
  233.4 2.2 collective-permute-done
  236.3 3.2 %constant_dynamic-update-slice_fusion.2 = (bf16[256,4352]{1,0:T(8,128)(2,1)}, bf16[256,896]{1,0:T(8,128)(2,1)S(1)}, f32[256,896]{1,0:T(8,128)S(1)}) fusion(bf16[256,4352]{1,0:T(8,128)(2,1)} %constant_dynamic-update-slice_fusion.3, f32[256,3328]{1,0:T(8,128)} %param.9, f32[]{:T(128)} %bitcast.7, bf16[256,3328]{1,0:T(8,128)(2,1)} %param.11, f32[]{:T(128)} %bitcast.6, ...), kind=kLoop, calls=%fused_computation.56 | loop fusion | flops 4358144 | bytes 4129792
  239.5 1.9 collective-permute-start.1
  241.5 3.0 %fusion.32 = (bf16[256,4352]{1,0:T(8,128)(2,1)}, f32[256,768]{1,0:T(8,128)S(1)}) fusion(bf16[256,4352]{1,0:T(8,128)(2,1)} %get-tuple-element.8, f32[256,3328]{1,0:T(8,128)} %param.9, f32[]{:T(128)} %bitcast.7, bf16[256,3328]{1,0:T(8,128)(2,1)} %param.11, f32[]{:T(128)} %bitcast.6, bf16[256,768]{1,0:T(8,128)(2,1)} %reduce-scatter.7.cloned.1.call-done, ...), kind=kLoop, calls=%fused_computation.50 | loop fusion | flops 3735552 | bytes 3146752
  244.4 6.5 %reduce-scatter.9.cloned.1.call-done = bf16[256,768]{1,0:T(8,128)(2,1)} async-done(((bf16[1024,768]{1,0:T(8,128)(2,1)}), bf16[256,768]{1,0:T(8,128)(2,1)}) %reduce-scatter.9.cloned.1.call-update) | async-done | bytes 393232 | tf_op jit(solution)/shard_map/reduce_scatter | solution.py:55
  250.9 3.0 %fusion.33 = (bf16[256,4352]{1,0:T(8,128)(2,1)}, f32[256,768]{1,0:T(8,128)S(1)}) fusion(bf16[256,4352]{1,0:T(8,128)(2,1)} %get-tuple-element.6, f32[256,3328]{1,0:T(8,128)} %param.9, f32[]{:T(128)} %bitcast.7, bf16[256,3328]{1,0:T(8,128)(2,1)} %param.11, f32[]{:T(128)} %bitcast.6, bf16[256,768]{1,0:T(8,128)(2,1)} %reduce-scatter.9.cloned.1.call-done, ...), kind=kLoop, calls=%fused_computation.51 | loop fusion | flops 3735552 | bytes 3146752
  253.9 2.0 pad_maximum_fusion
  256.7 2.4 dynamic-slice_select_fusion
  (33 shorter events, 10.5 us)
Async XLA Ops:
  7.2 44.2 %all-gather.2.cloned.1.call-start = ((), (), s32[]{:S(2)}) async-start(), calls=%async_computation.9 | async-start | bytes 2359296 | tf_op jit(solution)/shard_map/all_gather | solution.py:42
  31.0 48.4 %all-to-all-start.4 = ((bf16[8,128,896]{2,1,0:T(8,128)(2,1)}), bf16[8,128,896]{2,1,0:T(8,128)(2,1)}, u32[]{:S(2)}, u32[]{:S(2)}) async-start(bf16[8,128,896]{2,1,0:T(8,128)(2,1)} %stack.11), calls=%async_computation.7 | async-start | bytes 3670016 | tf_op jit(solution)/shard_map/all_to_all | solution.py:21
  80.9 50.4 %all-to-all-start.1 = ((bf16[8,128,896]{2,1,0:T(8,128)(2,1)}), bf16[8,128,896]{2,1,0:T(8,128)(2,1)}, u32[]{:S(2)}, u32[]{:S(2)}) async-start(bf16[8,128,896]{2,1,0:T(8,128)(2,1)} %stack.8), calls=%async_computation.1 | async-start | bytes 3670016 | tf_op jit(solution)/shard_map/all_to_all | solution.py:21
  85.2 141.8 %reduce-scatter.11.cloned.1.call-start = ((), (), s32[]{:S(2)}) async-start(), calls=%async_computation.13 | async-start | bytes 2293760 | tf_op jit(solution)/shard_map/reduce_scatter | solution.py:55
  90.4 145.9 %reduce-scatter.5.cloned.1.call-start = ((), (), s32[]{:S(2)}) async-start(), calls=%async_computation.10 | async-start | bytes 2293760 | tf_op jit(solution)/shard_map/reduce_scatter | solution.py:55
  180.5 41.2 %all-to-all-start.3 = ((bf16[8,128,768]{2,1,0:T(8,128)(2,1)}), bf16[8,128,768]{2,1,0:T(8,128)(2,1)}, u32[]{:S(2)}, u32[]{:S(2)}) async-start(bf16[8,128,768]{2,1,0:T(8,128)(2,1)} %stack.10), calls=%async_computation.5 | async-start | bytes 3145728 | tf_op jit(solution)/shard_map/all_to_all | solution.py:21
  184.8 56.7 %reduce-scatter.7.cloned.1.call-start = ((), (), s32[]{:S(2)}) async-start(), calls=%async_computation.11 | async-start | bytes 1966080 | tf_op jit(solution)/shard_map/reduce_scatter | solution.py:55
  189.3 61.6 %reduce-scatter.9.cloned.1.call-start = ((), (), s32[]{:S(2)}) async-start(), calls=%async_computation.12 | async-start | bytes 1966080 | tf_op jit(solution)/shard_map/reduce_scatter | solution.py:55
  226.2 5.3 %copy-start.1 = (s32[8]{0:T(128)S(1)}, s32[8]{0:T(128)}, u32[]{:S(2)}) copy-start(s32[8]{0:T(128)} %param.12) | copy-start | bytes 100
  229.4 6.3 %collective-permute-start = (bf16[256,256]{1,0:T(8,128)(2,1)S(1)}, bf16[256,256]{1,0:T(8,128)(2,1)S(1)}, u32[]{:S(2)}, u32[]{:S(2)}) collective-permute-start(bf16[256,256]{1,0:T(8,128)(2,1)S(1)} %slice.72), channel_id=1, source_target_pairs={{0,1},{1,2},{2,3},{3,4},{4,5},{5,6},{6,7},{8,9},{9,10},{10,11},{11... | collective-permute-start | bytes 393224 | tf_op jit(solution)/shard_map/ppermute | solution.py:70
  239.5 17.1 %collective-permute-start.1 = (bf16[256,256]{1,0:T(8,128)(2,1)S(1)}, bf16[256,256]{1,0:T(8,128)(2,1)S(1)}, u32[]{:S(2)}, u32[]{:S(2)}) collective-permute-start(bf16[256,256]{1,0:T(8,128)(2,1)S(1)} %slice.73), channel_id=1, source_target_pairs={{1,0},{2,1},{3,2},{4,3},{5,4},{6,5},{7,6},{9,8},{10,9},{11,10},{12... | collective-permute-start | bytes 393224 | tf_op jit(solution)/shard_map/ppermute | solution.py:71
  253.9 2.7 %copy-start = (bf16[256,4352]{1,0:T(8,128)(2,1)S(1)}, bf16[256,4352]{1,0:T(8,128)(2,1)}, u32[]{:S(2)}) copy-start(bf16[256,4352]{1,0:T(8,128)(2,1)} %get-tuple-element.4) | copy-start | bytes 6684676
Sparse Core Ops, SparseCore 0:
  28.6 22.7 all-gather.1
  90.5 31.6 reduce-scatter.10
  136.5 26.4 reduce-scatter.4
  189.4 29.7 reduce-scatter.6
  226.3 24.5 reduce-scatter.8
